TPU v7x, 32 devices: a whole 2x2x4 slice. The times are simulated.
32 devices in a mesh: dp: 8 (over y, x, core), tensor: 4 (over z).
Axes of the slice: x: 2, y: 2, z: 4, core: 2. Of those that a mesh axis runs over, the one named last changes fastest.
Arguments:
- tokens: bfloat16 [16384, 768], P('dp'), may hold values from -6 to 6
- cotangent: bfloat16 [16384, 768], P('dp'), may hold values from -6 to 6
- segment: int32 [32, 512], P('dp'), may hold values from 0 to 15, never falling along the last dimension, each value on 1 to 256 neighbouring positions
- box_x: int32 [32, 512], P('dp'), may hold values from 0 to 127
- box_y: int32 [32, 512], P('dp'), may hold values from 0 to 127
- page_tokens: int32 [32], P('dp'), may hold values from 128 to 512, as said below
- gain_attn: float32 [768], replicated, may hold values from 0.5 to 1.5
- shift_attn: float32 [768], replicated, may hold values from -3 to 3
- w_query: bfloat16 [768, 768], P(None, 'tensor'), may hold values from -0.21875 to 0.21875
- b_query: float32 [12, 64], P('tensor'), may hold values from -4 to 4
- w_key: bfloat16 [768, 768], P(None, 'tensor'), may hold values from -0.21875 to 0.21875
- w_value: bfloat16 [768, 768], P(None, 'tensor'), may hold values from -0.21875 to 0.21875
- b_value: float32 [12, 64], P('tensor'), may hold values from -4 to 4
- table_x: float32 [12, 64], P('tensor'), may hold values from -4 to 4
- table_y: float32 [12, 64], P('tensor'), may hold values from -4 to 4
- w_attn_out: bfloat16 [768, 768], P('tensor'), may hold values from -0.875 to 0.875
- b_attn_out: float32 [768], replicated, may hold values from -4 to 4
- gain_mlp: float32 [768], replicated, may hold values from 0.5 to 1.5
- shift_mlp: float32 [768], replicated, may hold values from -3 to 3
- w_in: bfloat16 [768, 3072], P(None, 'tensor'), may hold values from -0.21875 to 0.21875
- b_in: float32 [24, 128], P('tensor'), may hold values from -4 to 4
- w_out: bfloat16 [3072, 768], P('tensor'), may hold values from -0.109375 to 0.109375
- b_out: float32 [768], replicated, may hold values from -4 to 4
Outputs:
- layer_out: bfloat16 [16384, 768], P('dp')
- input_grad: bfloat16 [16384, 768], P('dp')
- grad_gain_attn: float32 [768], P('dp')
- grad_shift_attn: float32 [768], P('dp')
- grad_w_query: float32 [768, 768], P('dp', 'tensor')
- grad_b_query: float32 [12, 64], P('tensor', 'dp')
- grad_w_key: float32 [768, 768], P('dp', 'tensor')
- grad_w_value: float32 [768, 768], P('dp', 'tensor')
- grad_b_value: float32 [12, 64], P('tensor', 'dp')
- grad_table_x: float32 [12, 64], P('tensor', 'dp')
- grad_table_y: float32 [12, 64], P('tensor', 'dp')
- grad_w_attn_out: float32 [768, 768], P('tensor', 'dp')
- grad_b_attn_out: float32 [768], P('dp')
- grad_gain_mlp: float32 [768], P('dp')
- grad_shift_mlp: float32 [768], P('dp')
- grad_w_in: float32 [768, 3072], P('dp', 'tensor')
- grad_b_in: float32 [24, 128], P('tensor', 'dp')
- grad_w_out: float32 [3072, 768], P('tensor', 'dp')
- grad_b_out: float32 [768], P('dp')
Inputs may be any that keep to these rules, and one draw needn't show every extreme that they name: `page_tokens`: some page of every draw holds 512 tokens. Within a page the segment numbers never fall.
All inputs are finite; a program needn't handle non-finite values.
Results may differ from a plain program's by a relative error of at most 0.023.
Values may be sent and summed in bfloat16 or wider, within the bound.
No kernel may reach another device: no remote copies, remote signals or barrier semaphores. Data moves between devices by JAX's collectives and lax.ppermute only.
A program may use at most 192 MiB of HBM per device.

v0:
```python
from functools import partial

import jax
import jax.numpy as jnp
from jax import lax
from jax.sharding import PartitionSpec as P

BINS = 64
BOXES = 128


EPS = 1e-05
MASKED = -1e30
HIGH = lax.Precision.HIGHEST


def normalize(rows, gain, shift):
    mean = jnp.mean(rows, axis=-1, keepdims=True)
    centred = rows - mean
    inverse = lax.rsqrt(jnp.mean(centred * centred, axis=-1, keepdims=True) + EPS)
    unit = centred * inverse
    return (unit * gain + shift, unit, inverse)


def normalize_back(grad_out, unit, inverse, gain):
    scaled = grad_out * gain
    return inverse * (
        scaled
        - jnp.mean(scaled, axis=-1, keepdims=True)
        - unit * jnp.mean(scaled * unit, axis=-1, keepdims=True)
    )


def bucket_pick(boxes, bins):
    left = lax.broadcasted_iota(jnp.int32, (boxes, boxes), 0)
    right = lax.broadcasted_iota(jnp.int32, (boxes, boxes), 1)
    half = bins // 2
    bucket = jnp.clip(right - left, -half, half - 1) + half
    return (bucket[:, :, None] == jnp.arange(bins, dtype=jnp.int32)).astype(jnp.float32)


def page_bias(lookup_x, lookup_y, page_bx, page_by):
    levels = jnp.arange(lookup_x.shape[1], dtype=jnp.int32)
    onehot_x = (page_bx[:, None] == levels).astype(jnp.float32)
    onehot_y = (page_by[:, None] == levels).astype(jnp.float32)
    spread_x = jnp.einsum("ia,hac->hic", onehot_x, lookup_x, precision=HIGH)
    spread_y = jnp.einsum("ia,hac->hic", onehot_y, lookup_y, precision=HIGH)
    onehot = jnp.concatenate([onehot_x, onehot_y], axis=1).astype(jnp.bfloat16)
    spread = jnp.concatenate([spread_x, spread_y], axis=2)
    spread_high = spread.astype(jnp.bfloat16)
    spread_rest = (spread - spread_high.astype(jnp.float32)).astype(jnp.bfloat16)
    bias = jnp.einsum("hic,jc->hij", spread_high, onehot, preferred_element_type=jnp.float32)
    bias = bias + jnp.einsum("hic,jc->hij", spread_rest, onehot, preferred_element_type=jnp.float32)
    return (bias, onehot)


def page_mask(page_seg, length):
    place = jnp.arange(page_seg.shape[0], dtype=jnp.int32)
    valid = place < length
    return valid[None, :] & ((page_seg[:, None] == page_seg[None, :]) | ~valid[:, None])


def local(
    tokens,
    cotangent,
    segment,
    box_x,
    box_y,
    page_tokens,
    gain_attn,
    shift_attn,
    w_query,
    b_query,
    w_key,
    w_value,
    b_value,
    table_x,
    table_y,
    w_attn_out,
    b_attn_out,
    gain_mlp,
    shift_mlp,
    w_in,
    b_in,
    w_out,
    b_out,
):
    pages, page_len = segment.shape
    rows_all = tokens.shape[0]
    heads_here = table_x.shape[0]
    head_size = b_query.shape[1]
    inner = heads_here * head_size
    factor = head_size ** (-0.5)
    hidden = tokens.astype(jnp.float32)
    normed, unit_attn, inv_attn = normalize(hidden, gain_attn, shift_attn)
    normed_low = normed.astype(jnp.bfloat16)
    w_qkv = jnp.concatenate([w_query, w_key, w_value], axis=1)
    zero_bias = jnp.zeros((inner,), jnp.float32)
    qkv_bias = jnp.concatenate([b_query.reshape(-1), zero_bias, b_value.reshape(-1)])
    qkv = (jnp.dot(normed_low, w_qkv, preferred_element_type=jnp.float32) + qkv_bias).astype(
        jnp.bfloat16
    )
    shaped = (pages, page_len, heads_here, head_size)
    query = qkv[:, :inner].reshape(shaped)
    key_rows = qkv[:, inner : 2 * inner].reshape(shaped)
    value = qkv[:, 2 * inner :].reshape(shaped)
    pick = bucket_pick(BOXES, BINS)
    lookup_x = jnp.einsum("hb,acb->hac", table_x, pick, precision=HIGH)
    lookup_y = jnp.einsum("hb,acb->hac", table_y, pick, precision=HIGH)

    def page_scores(page_query, page_key, page_seg, page_bx, page_by, length):
        bias, onehot = page_bias(lookup_x, lookup_y, page_bx, page_by)
        allowed = page_mask(page_seg, length)
        scores = (
            jnp.einsum("ihd,jhd->hij", page_query, page_key, preferred_element_type=jnp.float32)
            * factor
            + bias
        )
        return (jnp.where(allowed[None], scores, MASKED), onehot)

    def page_forward(pieces):
        page_query, page_key, page_value, page_seg, page_bx, page_by, length = pieces
        scores, _ = page_scores(page_query, page_key, page_seg, page_bx, page_by, length)
        peak = jnp.max(scores, axis=-1, keepdims=True)
        raised = jnp.exp(scores - peak)
        total = jnp.sum(raised, axis=-1, keepdims=True)
        probs = (raised / total).astype(jnp.bfloat16)
        context = jnp.einsum("hij,jhd->ihd", probs, page_value, preferred_element_type=jnp.float32)
        return (context.astype(jnp.bfloat16), (peak + jnp.log(total))[:, :, 0])

    context, log_total = lax.map(
        page_forward, (query, key_rows, value, segment, box_x, box_y, page_tokens)
    )
    context = context.reshape(rows_all, inner)
    attn_part = jnp.dot(context, w_attn_out, preferred_element_type=jnp.float32).astype(
        jnp.bfloat16
    )
    grad_top = cotangent.astype(jnp.float32)
    attn_total = lax.psum(attn_part, "tensor").astype(jnp.float32)
    resid = hidden + (attn_total + b_attn_out)
    normed_two, unit_mlp, inv_mlp = normalize(resid, gain_mlp, shift_mlp)
    mlp_input = normed_two.astype(jnp.bfloat16)
    before = jnp.dot(mlp_input, w_in, preferred_element_type=jnp.float32) + b_in.reshape(-1)
    gelu_out, gelu_back = jax.vjp(partial(jax.nn.gelu, approximate=False), before)
    active = gelu_out.astype(jnp.bfloat16)
    mlp_part = jnp.dot(active, w_out, preferred_element_type=jnp.float32).astype(jnp.bfloat16)
    grad_w_out = jnp.einsum("tf,td->fd", active, cotangent, preferred_element_type=jnp.float32)
    grad_active = jnp.einsum("td,fd->tf", cotangent, w_out, preferred_element_type=jnp.float32)
    grad_before = gelu_back(grad_active)[0].astype(jnp.bfloat16)
    grad_w_in = jnp.einsum("td,tf->df", mlp_input, grad_before, preferred_element_type=jnp.float32)
    grad_b_in = jnp.sum(grad_before, axis=0, dtype=jnp.float32).reshape(b_in.shape)
    grad_mlp_part = jnp.einsum("tf,df->td", grad_before, w_in, preferred_element_type=jnp.float32)
    grad_b_out = jnp.sum(grad_top, axis=0)
    mlp_total = lax.psum(mlp_part, "tensor").astype(jnp.float32)
    layer_out = (resid + (mlp_total + b_out)).astype(jnp.bfloat16)
    grad_normed_mlp = lax.psum(grad_mlp_part.astype(jnp.bfloat16), "tensor").astype(jnp.float32)
    grad_resid = grad_top + normalize_back(grad_normed_mlp, unit_mlp, inv_mlp, gain_mlp)
    grad_branch = grad_resid.astype(jnp.bfloat16)
    grad_gain_mlp = jnp.sum(grad_normed_mlp * unit_mlp, axis=0)
    grad_shift_mlp = jnp.sum(grad_normed_mlp, axis=0)
    grad_b_attn_out = jnp.sum(grad_branch, axis=0, dtype=jnp.float32)
    grad_w_attn_out = jnp.einsum(
        "ti,td->id", context, grad_branch, preferred_element_type=jnp.float32
    )
    grad_context = jnp.einsum(
        "td,id->ti", grad_branch, w_attn_out, preferred_element_type=jnp.float32
    ).astype(jnp.bfloat16)

    def page_backward(pieces):
        (
            page_query,
            page_key,
            page_value,
            page_grad,
            page_seg,
            page_bx,
            page_by,
            length,
            page_total,
        ) = pieces
        scores, onehot = page_scores(page_query, page_key, page_seg, page_bx, page_by, length)
        probs = jnp.exp(scores - page_total[:, :, None])
        grad_value = jnp.einsum(
            "hij,ihd->jhd",
            probs.astype(jnp.bfloat16),
            page_grad,
            preferred_element_type=jnp.float32,
        )
        grad_probs = jnp.einsum(
            "ihd,jhd->hij", page_grad, page_value, preferred_element_type=jnp.float32
        )
        grad_scores = probs * (grad_probs - jnp.sum(probs * grad_probs, axis=-1, keepdims=True))
        low_scores = grad_scores.astype(jnp.bfloat16)
        grad_query = (
            jnp.einsum("hij,jhd->ihd", low_scores, page_key, preferred_element_type=jnp.float32)
            * factor
        )
        grad_key = (
            jnp.einsum("hij,ihd->jhd", low_scores, page_query, preferred_element_type=jnp.float32)
            * factor
        )
        grad_spread = jnp.einsum(
            "hij,jc->hic", low_scores, onehot, preferred_element_type=jnp.float32
        )
        levels = onehot.shape[1] // 2
        onehot_wide = onehot.astype(jnp.float32)
        grad_lookup_x = jnp.einsum(
            "ia,hic->hac", onehot_wide[:, :levels], grad_spread[:, :, :levels], precision=HIGH
        )
        grad_lookup_y = jnp.einsum(
            "ia,hic->hac", onehot_wide[:, levels:], grad_spread[:, :, levels:], precision=HIGH
        )
        return (
            grad_query.astype(jnp.bfloat16),
            grad_key.astype(jnp.bfloat16),
            grad_value.astype(jnp.bfloat16),
            grad_lookup_x,
            grad_lookup_y,
        )

    grad_q, grad_k, grad_v, grad_lx, grad_ly = lax.map(
        page_backward,
        (
            query,
            key_rows,
            value,
            grad_context.reshape(shaped),
            segment,
            box_x,
            box_y,
            page_tokens,
            log_total,
        ),
    )
    grad_table_x = jnp.einsum("hac,acb->hb", jnp.sum(grad_lx, axis=0), pick, precision=HIGH)
    grad_table_y = jnp.einsum("hac,acb->hb", jnp.sum(grad_ly, axis=0), pick, precision=HIGH)
    grad_q = grad_q.reshape(rows_all, inner)
    grad_v = grad_v.reshape(rows_all, inner)
    grad_qkv = jnp.concatenate([grad_q, grad_k.reshape(rows_all, inner), grad_v], axis=1)
    grad_b_query = jnp.sum(grad_q, axis=0, dtype=jnp.float32).reshape(heads_here, head_size)
    grad_b_value = jnp.sum(grad_v, axis=0, dtype=jnp.float32).reshape(heads_here, head_size)
    grad_w_qkv = jnp.einsum("td,tk->dk", normed_low, grad_qkv, preferred_element_type=jnp.float32)
    grad_attn_part = jnp.einsum("tk,dk->td", grad_qkv, w_qkv, preferred_element_type=jnp.float32)
    grad_normed_attn = lax.psum(grad_attn_part.astype(jnp.bfloat16), "tensor").astype(jnp.float32)
    input_grad = (
        grad_resid + normalize_back(grad_normed_attn, unit_attn, inv_attn, gain_attn)
    ).astype(jnp.bfloat16)
    grad_gain_attn = jnp.sum(grad_normed_attn * unit_attn, axis=0)
    grad_shift_attn = jnp.sum(grad_normed_attn, axis=0)
    vectors = jnp.stack(
        [
            grad_gain_attn,
            grad_shift_attn,
            grad_gain_mlp,
            grad_shift_mlp,
            grad_b_attn_out,
            grad_b_out,
        ]
    )
    head_bias = jnp.stack([grad_b_query, grad_b_value])
    head_table = jnp.stack([grad_table_x, grad_table_y])
    (
        summed_qkv,
        summed_attn_out,
        summed_in,
        summed_out,
        summed_vectors,
        summed_bias,
        summed_table,
        summed_b_in,
    ) = (
        lax.psum_scatter(grad_w_qkv, "dp", scatter_dimension=0, tiled=True),
        lax.psum_scatter(grad_w_attn_out, "dp", scatter_dimension=1, tiled=True),
        lax.psum_scatter(grad_w_in, "dp", scatter_dimension=0, tiled=True),
        lax.psum_scatter(grad_w_out, "dp", scatter_dimension=1, tiled=True),
        lax.psum_scatter(vectors, "dp", scatter_dimension=1, tiled=True),
        lax.psum_scatter(head_bias, "dp", scatter_dimension=2, tiled=True),
        lax.psum_scatter(head_table, "dp", scatter_dimension=2, tiled=True),
        lax.psum_scatter(grad_b_in, "dp", scatter_dimension=1, tiled=True),
    )
    return (
        layer_out,
        input_grad,
        summed_vectors[0],
        summed_vectors[1],
        summed_qkv[:, :inner],
        summed_bias[0],
        summed_qkv[:, inner : 2 * inner],
        summed_qkv[:, 2 * inner :],
        summed_bias[1],
        summed_table[0],
        summed_table[1],
        summed_attn_out,
        summed_vectors[4],
        summed_vectors[2],
        summed_vectors[3],
        summed_in,
        summed_b_in,
        summed_out,
        summed_vectors[5],
    )


def solution(mesh):
    return jax.shard_map(
        local,
        mesh=mesh,
        in_specs=(
            P("dp", None),
            P("dp", None),
            P("dp", None),
            P("dp", None),
            P("dp", None),
            P("dp"),
            P(),
            P(),
            P(None, "tensor"),
            P("tensor", None),
            P(None, "tensor"),
            P(None, "tensor"),
            P("tensor", None),
            P("tensor", None),
            P("tensor", None),
            P("tensor", None),
            P(),
            P(),
            P(),
            P(None, "tensor"),
            P("tensor", None),
            P("tensor", None),
            P(),
        ),
        out_specs=(
            P("dp", None),
            P("dp", None),
            P("dp"),
            P("dp"),
            P("dp", "tensor"),
            P("tensor", "dp"),
            P("dp", "tensor"),
            P("dp", "tensor"),
            P("tensor", "dp"),
            P("tensor", "dp"),
            P("tensor", "dp"),
            P("tensor", "dp"),
            P("dp"),
            P("dp"),
            P("dp"),
            P("dp", "tensor"),
            P("tensor", "dp"),
            P("tensor", "dp"),
            P("dp"),
        ),
        check_vma=False,
    )
```

profile of v0, /device:TPU:0, one launch (start us, length us, event | category | flops | bytes accessed | tf_op | source)
XLA Modules:
  0.0 929.4 jit_solution(3743095827307514756)
XLA Ops:
  17.7 4.3 add_convert_fusion.3
  35.0 32.5 %while.30 = (s32[]{:T(128)}, bf16[4,512,3,64]{1,3,2,0:T(8,128)(2,1)}, f32[4,3,512]{2,1,0:T(4,128)S(1)}, bf16[4,512,3,64]{1,3,2,0:T(8,128)(2,1)}, s32[4]{0:T(128)...) while((s32[]{:T(128)}, ...), condition=%wide.region_5.6_spmd, body=%wide.region_2.5_spmd.sunk | while | flops 1623948800 | bytes 28917920 | solution.py:131
  73.2 123.9 %all-reduce.8.cloned.1.call-done = bf16[2048,768]{1,0:T(8,128)(2,1)} async-done(((bf16[2048,768]{1,0:T(8,128)(2,1)}), bf16[2048,768]{1,0:T(8,128)(2,1)}) %all-reduce.8.cloned.1.call-update) | async-done | bytes 3145744 | tf_op jit(solution)/shard_map/psum | solution.py:139
  208.8 19.1 %convert_reduce_fusion.4 = (f32[768]{0:T(1024)}, bf16[2048,768]{1,0:T(8,128)(2,1)S(1)}, f32[2048,768]{1,0:T(8,128)}) fusion(f32[2048,768]{1,0:T(8,128)S(1)} %fusion.135, f32[768]{0:T(1024)S(1)} %bitcast.357, bf16[2048,768]{1,0:T(8,128)(2,1)S(1)} %copy-done.16, bf16[768,768]{1,0:T(8,128)(2,1)S(1)} %copy-done), kind=kOutput, calls=%fused_computation.141 | convolution fusion | flops 2533883136 | bytes 20060160 | tf_op jit(solution)/shard_map/td,fd->tf/dot_general | solution.py:148
  233.7 5.6 multiply_convert_fusion.1
  245.0 108.9 %all-reduce.10.cloned.1.call-done = bf16[2048,768]{1,0:T(8,128)(2,1)} async-done(((bf16[2048,768]{1,0:T(8,128)(2,1)}), bf16[2048,768]{1,0:T(8,128)(2,1)}) %all-reduce.10.cloned.1.call-update) | async-done | bytes 3145744 | tf_op jit(solution)/shard_map/psum | solution.py:156
  353.9 7.4 fusion.103
  361.3 5.3 convert_reduce_fusion.5
  377.0 65.5 %while.31 = (s32[]{:T(128)}, bf16[4,512,3,64]{1,3,2,0:T(8,128)(2,1)}, bf16[4,512,3,64]{1,3,2,0:T(8,128)(2,1)}, bf16[4,512,3,64]{1,3,2,0:T(8,128)(2,1)}, f32[4,3,...) while((s32[]{:T(128)}, ...), condition=%wide.region_15.16_spmd, body=%wide.region_13.15_spmd.sunk | while | flops 2934537728 | bytes 50130128 | solution.py:221
  447.6 4.3 convolution_convert_fusion.2
  453.4 5.1 convolution_bitcast_fusion.2
  458.5 6.5 fusion.127
  465.2 209.1 %all-reduce.12.cloned.1.call-done = (bf16[2048,768]{1,0:T(8,128)(2,1)}, bf16[2048,768]{1,0:T(8,128)(2,1)}) async-done(((bf16[2048,768]{1,0:T(8,128)(2,1)}, bf16[2048,768]{1,0:T(8,128)(2,1)}), (bf16[2048,768]{1,0:T(8,128)(2,1)}, bf16[2048,768]{1,0:T(8,128)(2,1)})) %all-reduce.12.cloned.1.call-update) | async-done | bytes 6291472 | tf_op jit(solution)/shard_map/psum | solution.py:154
  674.3 5.7 fusion.104
  681.0 7.0 fusion.136
  688.4 7.1 fusion.137
  696.8 13.1 %reduce-scatter.25.cloned.1.call-done = f32[16,6]{1,0:T(8,128)} async-done(((f32[128,6]{1,0:T(8,128)}), f32[16,6]{1,0:T(8,128)}) %reduce-scatter.25.cloned.1.call-update) | async-done | bytes 400
  717.8 12.5 %all-reduce.2 = (f32[2,3,64]{2,1,0:T(4,128)S(1)}, f32[2,3,64]{2,1,0:T(4,128)S(1)}) all-reduce(f32[2,3,64]{2,1,0:T(4,128)S(1)} %pad_maximum_fusion.3, f32[2,3,64]{2,1,0:T(4,128)S(1)} %pad_maximum_fusion.4), channel_id=4, replica_groups=mesh['dp'=8,'tensor'=4] {'dp'}, use_global_device_ids=true, to_apply=%region_29.30.clone | all-reduce | flops 768 | bytes 6144
  731.5 16.7 %reduce-scatter.23.cloned.1.call-done = f32[96,192]{1,0:T(8,128)} async-done(((f32[768,192]{1,0:T(8,128)}), f32[96,192]{1,0:T(8,128)}) %reduce-scatter.23.cloned.1.call-update) | async-done | bytes 73744
  749.9 42.3 %reduce-scatter.15.cloned.1.call-done = f32[96,576]{1,0:T(8,128)} async-done(((f32[768,576]{1,0:T(8,128)}), f32[96,576]{1,0:T(8,128)}) %reduce-scatter.15.cloned.1.call-update) | async-done | bytes 221200 | tf_op jit(solution)/shard_map/reduce_scatter | solution.py:272
  795.4 11.3 %fusion.96 = (bf16[2048,768]{1,0:T(8,128)(2,1)}, bf16[2048,768]{1,0:T(8,128)(2,1)}) fusion(f32[2048,768]{1,0:T(8,128)} %copy-done.6, bf16[2048,768]{1,0:T(8,128)(2,1)} %param.27, bf16[2048,768]{1,0:T(8,128)(2,1)} %get-tuple-element.336, f32[2048]{0:T(1024)S(1)} %broadcast_multiply_fusion, f32[2048]{0:T(1024)S(1)} %broadcast_multiply_fusion.1, ...), kind=kLoop, calls=%fused_computation.132 | loop fusion | flops 28311552 | bytes 25207808 | tf_op jit(solution)/shard_map/convert_element_type | solution.py:247
  806.7 22.4 %reduce-scatter.21.cloned.1.call-done = f32[96,6]{1,0:T(8,128)} async-done(((f32[768,6]{1,0:T(8,128)}), f32[96,6]{1,0:T(8,128)}) %reduce-scatter.21.cloned.1.call-update) | async-done | bytes 2320
  833.8 41.7 %reduce-scatter.17.cloned.1.call-done = f32[96,768]{1,0:T(8,128)} async-done(((f32[768,768]{1,0:T(8,128)}), f32[96,768]{1,0:T(8,128)}) %reduce-scatter.17.cloned.1.call-update) | async-done | bytes 294928 | tf_op jit(solution)/shard_map/reduce_scatter | solution.py:274
  875.6 46.8 %reduce-scatter.19.cloned.1.call-done = f32[768,96]{0,1:T(8,128)} async-done(((f32[768,768]{0,1:T(8,128)}), f32[768,96]{0,1:T(8,128)}) %reduce-scatter.19.cloned.1.call-update) | async-done | bytes 294928 | tf_op jit(solution)/shard_map/reduce_scatter | solution.py:275
  (350 shorter events, 186.5 us)
Async XLA Ops:
  7.2 201.4 %copy-start = (bf16[768,768]{1,0:T(8,128)(2,1)S(1)}, bf16[768,768]{1,0:T(8,128)(2,1)}, u32[]{:S(2)}) copy-start(bf16[768,768]{1,0:T(8,128)(2,1)} %param.48) | copy-start | bytes 3538948
  7.3 189.8 %all-reduce.8.cloned.1.call-start = ((), (), s32[]{:S(2)}) async-start(), calls=%async_computation.6 | async-start | bytes 6291456 | tf_op jit(solution)/shard_map/psum | solution.py:139
  23.2 11.8 %copy-start.31 = (s32[4,512]{1,0:T(4,128)S(1)}, s32[4,512]{1,0:T(4,128)}, u32[]{:S(2)}) copy-start(s32[4,512]{1,0:T(4,128)} %param.30) | copy-start | bytes 24580
  23.2 11.8 %copy-start.32 = (s32[4,512]{1,0:T(4,128)S(1)}, s32[4,512]{1,0:T(4,128)}, u32[]{:S(2)}) copy-start(s32[4,512]{1,0:T(4,128)} %param.31) | copy-start | bytes 24580
  23.2 11.8 %copy-start.33 = (s32[4,512]{1,0:T(4,128)S(1)}, s32[4,512]{1,0:T(4,128)}, u32[]{:S(2)}) copy-start(s32[4,512]{1,0:T(4,128)} %param.29) | copy-start | bytes 24580
  23.2 11.8 %copy-start.45 = (s32[4]{0:T(128)S(1)}, s32[4]{0:T(128)}, u32[]{:S(2)}) copy-start(s32[4]{0:T(128)} %param.32) | copy-start | bytes 52
  35.0 35.4 %copy-start.17 = (bf16[192,768]{1,0:T(8,128)(2,1)S(1)}, bf16[192,768]{1,0:T(8,128)(2,1)}, u32[]{:S(2)}) copy-start(bf16[192,768]{1,0:T(8,128)(2,1)} %param.42) | copy-start | bytes 884740
  69.3 127.7 %copy-start.23 = (f32[768]{0:T(1024)S(1)}, f32[768]{0:T(1024)}, u32[]{:S(2)}) copy-start(f32[768]{0:T(1024)} %param.43) | copy-start | bytes 9220
  73.1 130.8 %copy-start.34 = (f32[768]{0:T(1024)S(1)}, f32[768]{0:T(1024)}, u32[]{:S(2)}) copy-start(f32[768]{0:T(1024)} %param.44) | copy-start | bytes 9220
  73.1 130.8 %copy-start.37 = (f32[768]{0:T(1024)S(1)}, f32[768]{0:T(1024)}, u32[]{:S(2)}) copy-start(f32[768]{0:T(1024)} %param.45) | copy-start | bytes 9220
  73.2 280.8 %all-reduce.10.cloned.1.call-start = ((), (), s32[]{:S(2)}) async-start(), calls=%async_computation.7 | async-start | bytes 6291456 | tf_op jit(solution)/shard_map/psum | solution.py:156
  208.6 19.4 %copy-start.12 = (f32[2048,768]{1,0:T(8,128)}, f32[2048,768]{1,0:T(8,128)S(1)}, u32[]{:S(2)}) copy-start(f32[2048,768]{1,0:T(8,128)S(1)} %fusion.135) | copy-start | bytes 18874372
  233.7 440.6 %all-reduce.12.cloned.1.call-start = ((), (), s32[]{:S(2)}) async-start(), calls=%async_computation.14 | async-start | bytes 12582912 | tf_op jit(solution)/shard_map/psum | solution.py:154
  451.9 258.0 %reduce-scatter.25.cloned.1.call-start = ((), (), s32[]{:S(2)}) async-start(), calls=%async_computation.13 | async-start | bytes 73728
  453.3 294.9 %reduce-scatter.23.cloned.1.call-start = ((), (), s32[]{:S(2)}) async-start(), calls=%async_computation.12 | async-start | bytes 884736
  458.4 333.8 %reduce-scatter.15.cloned.1.call-start = ((), (), s32[]{:S(2)}) async-start(), calls=%async_computation.8 | async-start | bytes 2211840 | tf_op jit(solution)/shard_map/reduce_scatter | solution.py:272
  465.1 364.0 %reduce-scatter.21.cloned.1.call-start = ((), (), s32[]{:S(2)}) async-start(), calls=%async_computation.11 | async-start | bytes 442368
  681.0 194.6 %reduce-scatter.17.cloned.1.call-start = ((), (), s32[]{:S(2)}) async-start(), calls=%async_computation.9 | async-start | bytes 2654208 | tf_op jit(solution)/shard_map/reduce_scatter | solution.py:274
  688.1 23.2 %copy-start.18 = (f32[4,3,128,128]{2,3,1,0:T(8,128)S(1)}, f32[4,3,128,128]{2,3,1,0:T(8,128)}, u32[]{:S(2)}) copy-start(f32[4,3,128,128]{2,3,1,0:T(8,128)} %get-tuple-element.179) | copy-start | bytes 2359300
  688.1 23.2 %copy-start.19 = (f32[4,3,128,128]{2,3,1,0:T(8,128)S(1)}, f32[4,3,128,128]{2,3,1,0:T(8,128)}, u32[]{:S(2)}) copy-start(f32[4,3,128,128]{2,3,1,0:T(8,128)} %get-tuple-element.178) | copy-start | bytes 2359300
  688.1 23.6 %copy-start.11 = (bf16[4,512,3,64]{1,3,2,0:T(8,128)(2,1)S(1)}, bf16[4,512,3,64]{1,3,2,0:T(8,128)(2,1)}, u32[]{:S(2)}) copy-start(bf16[4,512,3,64]{1,3,2,0:T(8,128)(2,1)} %get-tuple-element.175) | copy-start | bytes 2359300
  688.1 234.3 %reduce-scatter.19.cloned.1.call-start = ((), (), s32[]{:S(2)}) async-start(), calls=%async_computation.10 | async-start | bytes 2654208 | tf_op jit(solution)/shard_map/reduce_scatter | solution.py:275
  695.5 16.4 %copy-start.10 = (bf16[4,512,3,64]{1,3,2,0:T(8,128)(2,1)S(1)}, bf16[4,512,3,64]{1,3,2,0:T(8,128)(2,1)}, u32[]{:S(2)}) copy-start(bf16[4,512,3,64]{1,3,2,0:T(8,128)(2,1)} %get-tuple-element.177) | copy-start | bytes 2359300
  795.4 127.0 %copy-start.1 = (bf16[768,768]{1,0:T(8,128)(2,1)S(1)}, bf16[768,768]{1,0:T(8,128)(2,1)}, u32[]{:S(2)}) copy-start(bf16[768,768]{1,0:T(8,128)(2,1)} %param.48) | copy-start | bytes 3538948
  (33 other events, 182.3 us)
Sparse Core Ops, SparseCore 0:
  73.3 123.7 all-reduce.7
  233.8 120.0 all-reduce.9
  452.0 222.2 all-reduce.11
  677.7 32.1 reduce-scatter.24
  713.2 34.9 reduce-scatter.22
  751.9 40.2 reduce-scatter.14
  795.3 33.7 reduce-scatter.20
  833.0 42.4 reduce-scatter.16
  879.8 42.4 reduce-scatter.18
where the time goes:
time: 937 us; the launch traced here: 929 us
  waiting for transfers between devices  625 us (67%)
  matrix products  154 us (16%)
  other arithmetic  65.4 us (7%)
  local copies, waits for them, and re-layouts  55.1 us (6%)
  between operations  15.8 us (2%)
  blocking collectives  12.5 us (1%)
    psum x1, waiting for transfers between devices, local(): mlp_total = lax.psum(mlp_part, 'tensor').astype(jnp.float32)  209 us
    psum x1, waiting for transfers between devices, local(): attn_total = lax.psum(attn_part, 'tensor').astype(jnp.float32)  124 us
    psum x1, waiting for transfers between devices, local(): lax.psum(grad_mlp_part.astype(jnp.bfloat16), 'tensor').astype(jnp.float32)  109 us
    unnamed x12, waiting for transfers between devices  52.4 us
    reduce_scatter x1, waiting for transfers between devices, local(): lax.psum_scatter(grad_w_out, 'dp', scatter_dimension=1, tiled=True)  46.8 us
    reduce_scatter x1, waiting for transfers between devices, local(): lax.psum_scatter(grad_w_qkv, 'dp', scatter_dimension=0, tiled=True)  42.3 us
    reduce_scatter x1, waiting for transfers between devices, local(): lax.psum_scatter(grad_w_in, 'dp', scatter_dimension=0, tiled=True)  41.7 us
    dot_general x1, matrix products, local(): jnp.einsum('td,fd->tf', cotangent, w_out, preferred_element_type=jnp.floa...  19.1 us
  transfers between devices with their start and end apart: 9, of which 9 were waited for; matrix products, arithmetic and copies ran while one was open for 8% of the time, Pallas kernels for 0%

commit v1 on v0

v1 whole, which is shorter than its diff:
```python
import jax
import jax.numpy as jnp
from jax import lax
from jax.experimental import pallas as pl
from jax.experimental.pallas import tpu as pltpu
from jax.sharding import PartitionSpec as P

LEVELS = 128
BINS = 64
SEGS = 16
GROUP = 8
EPS = 1e-05
BARRED = -1e30
F32 = jnp.float32
BF16 = jnp.bfloat16
VMEM_BYTES = 56 * 1024 * 1024

NN = (((1,), (0,)), ((), ()))
NT = (((1,), (1,)), ((), ()))
TN = (((0,), (0,)), ((), ()))


def mm(left, right, dims=NN):
    return lax.dot_general(left, right, dims, preferred_element_type=F32)


def norm_stats(rows):
    mean = jnp.mean(rows, axis=-1, keepdims=True)
    centred = rows - mean
    inverse = lax.rsqrt(jnp.mean(centred * centred, axis=-1, keepdims=True) + EPS)
    return centred * inverse, inverse


def norm_back(grad_out, unit, inverse, gain):
    scaled = grad_out * gain
    return inverse * (
        scaled
        - jnp.mean(scaled, axis=-1, keepdims=True)
        - unit * jnp.mean(scaled * unit, axis=-1, keepdims=True)
    )


def page_columns(seg_row, bx_row, by_row):
    count = seg_row.shape[1]
    rows = jnp.concatenate(
        [seg_row.astype(F32), bx_row.astype(F32), by_row.astype(F32), jnp.zeros((5, count), F32)],
        axis=0,
    )
    columns = jnp.transpose(rows).astype(jnp.int32)
    return columns[:, 0:1], columns[:, 1:2], columns[:, 2:3]


def segment_terms(seg_col, length):
    count = seg_col.shape[0]
    lane = lax.broadcasted_iota(jnp.int32, (count, 64), 1)
    place = lax.broadcasted_iota(jnp.int32, (count, 64), 0)
    valid = place < length
    same = seg_col == lane
    query_side = jnp.where(valid, jnp.where(same, 1.0, 0.0), jnp.where(lane == SEGS, 1.0, 0.0))
    key_side = jnp.where(
        valid,
        jnp.where(same | (lane >= SEGS), 0.0, BARRED),
        jnp.where(lane <= SEGS, BARRED, 0.0),
    )
    return query_side.astype(BF16), key_side.astype(BF16)


def level_onehot(column):
    count = column.shape[0]
    lane = lax.broadcasted_iota(jnp.int32, (count, LEVELS), 1)
    return jnp.where(column == lane, 1.0, 0.0).astype(BF16)


def level_onehot_t(row):
    count = row.shape[1]
    level = lax.broadcasted_iota(jnp.int32, (LEVELS, count), 0)
    return jnp.where(row == level, 1.0, 0.0).astype(BF16)


def lookup_pair(offsets_row):
    wide = jnp.broadcast_to(offsets_row, (LEVELS, 2 * LEVELS))
    table = pltpu.roll(wide, 0, 1, stride=1, stride_axis=0)[:, LEVELS:]
    high = table.astype(BF16)
    rest = (table - high.astype(F32)).astype(BF16)
    return jnp.concatenate([high, rest], axis=1)


def attn_forward_kernel(
    lengths, tokens, seg, bx, by, gain, shift, weights, bias, offsets, context, looks, q_side, k_side
):
    step = pl.program_id(0)
    heads = looks.shape[0]
    size = weights.shape[1] // 3 // heads
    inner = heads * size

    @pl.when(step == 0)
    def _():
        for h in range(heads):
            looks[h, 0] = lookup_pair(offsets[h, 0:1, :])
            looks[h, 1] = lookup_pair(offsets[h, 1:2, :])

    unit, _ = norm_stats(tokens[0].astype(F32))
    normed = (unit * gain[...] + shift[...]).astype(BF16)
    qkv = (mm(normed, weights[...]) + bias[...]).astype(BF16)
    seg_col, bx_col, by_col = page_columns(seg[0], bx[0], by[0])
    seg_q, seg_k = segment_terms(seg_col, lengths[step])
    hot_x = level_onehot(bx_col)
    hot_y = level_onehot(by_col)
    k_side[:, 128:256] = hot_x
    k_side[:, 256:384] = hot_x
    k_side[:, 384:512] = hot_y
    k_side[:, 512:640] = hot_y
    factor = jnp.asarray(size ** (-0.5), BF16)
    ones = jnp.ones((qkv.shape[0], size), BF16)
    results = []
    for h in range(heads):
        query = qkv[:, h * size : (h + 1) * size] * factor
        key = qkv[:, inner + h * size : inner + (h + 1) * size]
        value = qkv[:, 2 * inner + h * size : 2 * inner + (h + 1) * size]
        q_side[:, 0:128] = jnp.concatenate([query, seg_q], axis=1)
        k_side[:, 0:128] = jnp.concatenate([key, seg_k], axis=1)
        q_side[:, 128:384] = mm(hot_x, looks[h, 0]).astype(BF16)
        q_side[:, 384:640] = mm(hot_y, looks[h, 1]).astype(BF16)
        scores = mm(q_side[...], k_side[...], NT)
        peak = jnp.max(scores, axis=1, keepdims=True)
        raised = jnp.exp(scores - peak).astype(BF16)
        both = mm(raised, jnp.concatenate([value, ones], axis=1))
        results.append(both[:, :size] / both[:, size : size + 1])
    context[0] = jnp.concatenate(results, axis=1).astype(BF16)


def attn_forward(lengths, tokens, seg, bx, by, gain, shift, weights, bias, offsets):
    pages, count, width = tokens.shape
    heads = offsets.shape[0]
    inner = weights.shape[1] // 3
    row = pl.BlockSpec((1, 1, count), lambda p, n: (p, 0, 0))
    whole = lambda shape: pl.BlockSpec(shape, lambda p, n: (0,) * len(shape))
    return pl.pallas_call(
        attn_forward_kernel,
        out_shape=jax.ShapeDtypeStruct((pages, count, inner), BF16),
        grid_spec=pltpu.PrefetchScalarGridSpec(
            num_scalar_prefetch=1,
            grid=(pages,),
            in_specs=[
                pl.BlockSpec((1, count, width), lambda p, n: (p, 0, 0)),
                row,
                row,
                row,
                whole((1, width)),
                whole((1, width)),
                whole((width, 3 * inner)),
                whole((1, 3 * inner)),
                whole((heads, 8, 2 * LEVELS)),
            ],
            out_specs=pl.BlockSpec((1, count, inner), lambda p, n: (p, 0, 0)),
            scratch_shapes=[
                pltpu.VMEM((heads, 2, LEVELS, 2 * LEVELS), BF16),
                pltpu.VMEM((count, 640), BF16),
                pltpu.VMEM((count, 640), BF16),
            ],
        ),
        compiler_params=pltpu.CompilerParams(vmem_limit_bytes=VMEM_BYTES),
        name="attn_forward",
    )(lengths, tokens, seg, bx, by, gain, shift, weights, bias, offsets)


def mlp_kernel(
    tokens,
    cotangent,
    context,
    w_attn,
    b_attn,
    gain,
    shift,
    w_in,
    b_in,
    w_out,
    b_out,
    layer_out,
    grad_resid,
    grads,
    rows_out,
    grad_b_in,
    resid,
    low,
    low_t,
    cot_t,
    out_sum,
    back_sum,
):
    step = pl.program_id(0)
    count, width = resid.shape
    hidden = w_in.shape[3]

    @pl.when(step == 0)
    def _():
        total = b_attn[...]
        for t in range(context.shape[0]):
            piece = w_attn[:, t].reshape(width, context.shape[2])
            total = total + mm(context[t], piece, NT)
        resid[...] = tokens[...].astype(F32) + total
        unit, _ = norm_stats(resid[...])
        normed = (unit * gain[...] + shift[...]).astype(BF16)
        low[...] = normed
        low_t[...] = jnp.transpose(normed)
        cot_t[...] = jnp.transpose(cotangent[...])
        out_sum[...] = jnp.zeros_like(out_sum)
        back_sum[...] = jnp.zeros_like(back_sum)

    w_up = w_in[:, 0].reshape(width, hidden)
    w_down = w_out[:, 0].reshape(hidden, width)
    before = mm(low[...], w_up) + b_in[0]
    half = 0.5 * (1.0 + lax.erf(before * (0.5**0.5)))
    active = (before * half).astype(BF16)
    slope = half + before * (jnp.exp(-0.5 * before * before) * 0.3989422804014327)
    out_sum[...] += mm(active, w_down)
    grad_before = (mm(cotangent[...], w_down, NT) * slope).astype(BF16)
    back_sum[...] += mm(grad_before, w_up, NT)
    grads[:, 0, 0] = mm(low_t[...], grad_before).astype(BF16).reshape(grads.shape[0], -1, hidden)
    grads[:, 0, 1] = mm(cot_t[...], active).astype(BF16).reshape(grads.shape[0], -1, hidden)
    grad_b_in[0] = jnp.sum(grad_before.astype(F32), axis=0, keepdims=True)

    @pl.when(step == pl.num_programs(0) - 1)
    def _():
        top = cotangent[...].astype(F32)
        layer_out[...] = (resid[...] + (out_sum[...] + b_out[...])).astype(BF16)
        unit, inverse = norm_stats(resid[...])
        back = back_sum[...]
        grad = top + norm_back(back, unit, inverse, gain[...])
        grad_resid[...] = grad
        rows_out[...] = jnp.concatenate(
            [
                jnp.sum(back * unit, axis=0, keepdims=True),
                jnp.sum(back, axis=0, keepdims=True),
                jnp.sum(grad.astype(BF16).astype(F32), axis=0, keepdims=True),
                jnp.sum(top, axis=0, keepdims=True),
                jnp.zeros((4, width), F32),
            ],
            axis=0,
        )


def mlp(tokens, cotangent, context, w_attn, b_attn, gain, shift, w_in, b_in, w_out, b_out):
    count, width = tokens.shape
    parts, groups, piece, hidden = w_in.shape
    whole = lambda shape: pl.BlockSpec(shape, lambda g: (0,) * len(shape))
    chunk = pl.BlockSpec((parts, 1, piece, hidden), lambda g: (0, g, 0, 0))
    return pl.pallas_call(
        mlp_kernel,
        out_shape=(
            jax.ShapeDtypeStruct((count, width), BF16),
            jax.ShapeDtypeStruct((count, width), F32),
            jax.ShapeDtypeStruct((GROUP, groups, 2, width // GROUP, hidden), BF16),
            jax.ShapeDtypeStruct((8, width), F32),
            jax.ShapeDtypeStruct((groups, 1, hidden), F32),
        ),
        grid_spec=pltpu.PrefetchScalarGridSpec(
            num_scalar_prefetch=0,
            grid=(groups,),
            in_specs=[
                whole(tokens.shape),
                whole(cotangent.shape),
                whole(context.shape),
                whole(w_attn.shape),
                whole((1, width)),
                whole((1, width)),
                whole((1, width)),
                chunk,
                pl.BlockSpec((1, 1, hidden), lambda g: (g, 0, 0)),
                chunk,
                whole((1, width)),
            ],
            out_specs=(
                whole((count, width)),
                whole((count, width)),
                pl.BlockSpec(
                    (GROUP, 1, 2, width // GROUP, hidden), lambda g: (0, g, 0, 0, 0)
                ),
                whole((8, width)),
                pl.BlockSpec((1, 1, hidden), lambda g: (g, 0, 0)),
            ),
            scratch_shapes=[
                pltpu.VMEM((count, width), F32),
                pltpu.VMEM((count, width), BF16),
                pltpu.VMEM((width, count), BF16),
                pltpu.VMEM((width, count), BF16),
                pltpu.VMEM((count, width), F32),
                pltpu.VMEM((count, width), F32),
            ],
        ),
        compiler_params=pltpu.CompilerParams(vmem_limit_bytes=VMEM_BYTES),
        name="mlp",
    )(tokens, cotangent, context, w_attn, b_attn, gain, shift, w_in, b_in, w_out, b_out)


def attn_backward_kernel(
    lengths,
    tokens,
    grad_resid,
    context,
    seg,
    bx,
    by,
    gain,
    shift,
    weights,
    bias,
    offsets,
    input_grad,
    grads,
    rows_out,
    bias_out,
    table_out,
    low,
    low_t,
    branch,
    branch_t,
    back_sum,
    hot,
    hot_t,
    q_side,
    k_side,
):
    step = pl.program_id(0)
    count, width = low.shape
    heads = offsets.shape[1]
    inner = context.shape[2]
    size = inner // heads

    @pl.when(step == 0)
    def _():
        unit, _ = norm_stats(tokens[...].astype(F32))
        normed = (unit * gain[...] + shift[...]).astype(BF16)
        low[...] = normed
        low_t[...] = jnp.transpose(normed)
        rounded = grad_resid[...].astype(BF16)
        branch[...] = rounded
        branch_t[...] = jnp.transpose(rounded)
        back_sum[...] = jnp.zeros_like(back_sum)
        seg_col, bx_col, by_col = page_columns(seg[...], bx[...], by[...])
        seg_q, seg_k = segment_terms(seg_col, lengths[0])
        hot_x = level_onehot(bx_col)
        hot_y = level_onehot(by_col)
        hot[:, 0:128] = level_onehot(LEVELS - 1 - bx_col)
        hot[:, 128:256] = level_onehot(LEVELS - 1 - by_col)
        hot_t[0:128, :] = level_onehot_t(bx[...])
        hot_t[128:256, :] = level_onehot_t(by[...])
        q_side[:, 0:128] = jnp.concatenate([seg_q, seg_q], axis=1)
        k_side[:, 0:128] = jnp.concatenate([seg_k, seg_k], axis=1)
        k_side[:, 128:256] = hot_x
        k_side[:, 256:384] = hot_x
        k_side[:, 384:512] = hot_y
        k_side[:, 512:640] = hot_y

    w_all = weights[:, 0].reshape(width, 4 * inner)
    w_qkv = w_all[:, : 3 * inner]
    qkv = (mm(low[...], w_qkv) + bias[0]).astype(BF16)
    grad_ctx = mm(branch[...], w_all[:, 3 * inner :]).astype(BF16)
    factor = jnp.asarray(size ** (-0.5), BF16)
    grad_q, grad_k, grad_v = [], [], []
    for h in range(heads):
        query = qkv[:, h * size : (h + 1) * size] * factor
        key = qkv[:, inner + h * size : inner + (h + 1) * size]
        value = qkv[:, 2 * inner + h * size : 2 * inner + (h + 1) * size]
        grad_here = grad_ctx[:, h * size : (h + 1) * size]
        q_side[:, 0:size] = query
        k_side[:, 0:size] = key
        q_side[:, 128:384] = mm(k_side[:, 128:256], lookup_pair(offsets[0, h, 0:1, :])).astype(BF16)
        q_side[:, 384:640] = mm(k_side[:, 384:512], lookup_pair(offsets[0, h, 1:2, :])).astype(BF16)
        scores = mm(k_side[...], q_side[...], NT)
        raised = jnp.exp(scores - jnp.max(scores, axis=0, keepdims=True))
        probs = raised * (1.0 / jnp.sum(raised, axis=0, keepdims=True))
        grad_v.append(mm(probs.astype(BF16), grad_here))
        weighted = probs * mm(value, grad_here, NT)
        grad_scores = weighted - probs * jnp.sum(weighted, axis=0, keepdims=True)
        low_scores = grad_scores.astype(BF16)
        grad_k.append(mm(low_scores, query))
        grad_q.append(jnp.transpose(mm(key, low_scores, TN)) * (size ** (-0.5)))
        spread = mm(low_scores, hot[...]).astype(BF16)
        for axis in range(2):
            lanes = slice(axis * LEVELS, (axis + 1) * LEVELS)
            square = mm(hot_t[lanes, :], spread[:, lanes])
            wide = jnp.concatenate([square, jnp.zeros_like(square)], axis=1)
            turned = pltpu.roll(wide, 0, 1, stride=1, stride_axis=0)
            table_out[0, h, axis : axis + 1, :] = jnp.sum(turned, axis=0, keepdims=True)
    grad_q = jnp.concatenate(grad_q, axis=1).astype(BF16)
    grad_k = jnp.concatenate(grad_k, axis=1).astype(BF16)
    grad_v = jnp.concatenate(grad_v, axis=1).astype(BF16)
    bias_out[0] = jnp.concatenate(
        [
            jnp.sum(grad_q.astype(F32), axis=0, keepdims=True),
            jnp.sum(grad_v.astype(F32), axis=0, keepdims=True),
            jnp.zeros((6, inner), F32),
        ],
        axis=0,
    )
    grad_qkv = jnp.concatenate([grad_q, grad_k, grad_v], axis=1)
    back_sum[...] += mm(grad_qkv, w_qkv, NT)
    grads[:, 0] = (
        jnp.concatenate(
            [mm(low_t[...], grad_qkv), mm(branch_t[...], context[0])], axis=1
        )
        .astype(BF16)
        .reshape(grads.shape[0], -1, 4 * inner)
    )

    @pl.when(step == pl.num_programs(0) - 1)
    def _():
        back = back_sum[...]
        unit, inverse = norm_stats(tokens[...].astype(F32))
        input_grad[...] = (grad_resid[...] + norm_back(back, unit, inverse, gain[...])).astype(BF16)
        rows_out[...] = jnp.concatenate(
            [
                jnp.sum(back * unit, axis=0, keepdims=True),
                jnp.sum(back, axis=0, keepdims=True),
                jnp.zeros((6, width), F32),
            ],
            axis=0,
        )


def attn_backward(
    length, tokens, grad_resid, context, seg, bx, by, gain, shift, weights, bias, offsets
):
    count, width = tokens.shape
    groups, _, inner = context.shape
    heads = offsets.shape[1]
    parts, _, piece, _ = weights.shape
    whole = lambda shape: pl.BlockSpec(shape, lambda g, n: (0,) * len(shape))
    return pl.pallas_call(
        attn_backward_kernel,
        out_shape=(
            jax.ShapeDtypeStruct((count, width), BF16),
            jax.ShapeDtypeStruct((GROUP, groups, width // GROUP, 4 * inner), BF16),
            jax.ShapeDtypeStruct((8, width), F32),
            jax.ShapeDtypeStruct((groups, 8, inner), F32),
            jax.ShapeDtypeStruct((groups, heads, 8, 2 * LEVELS), F32),
        ),
        grid_spec=pltpu.PrefetchScalarGridSpec(
            num_scalar_prefetch=1,
            grid=(groups,),
            in_specs=[
                whole((count, width)),
                whole((count, width)),
                pl.BlockSpec((1, count, inner), lambda g, n: (g, 0, 0)),
                whole((1, count)),
                whole((1, count)),
                whole((1, count)),
                whole((1, width)),
                whole((1, width)),
                pl.BlockSpec((parts, 1, piece, 4 * inner), lambda g, n: (0, g, 0, 0)),
                pl.BlockSpec((1, 1, 3 * inner), lambda g, n: (g, 0, 0)),
                pl.BlockSpec((1, heads, 8, 2 * LEVELS), lambda g, n: (g, 0, 0, 0)),
            ],
            out_specs=(
                whole((count, width)),
                pl.BlockSpec((GROUP, 1, width // GROUP, 4 * inner), lambda g, n: (0, g, 0, 0)),
                whole((8, width)),
                pl.BlockSpec((1, 8, inner), lambda g, n: (g, 0, 0)),
                pl.BlockSpec((1, heads, 8, 2 * LEVELS), lambda g, n: (g, 0, 0, 0)),
            ),
            scratch_shapes=[
                pltpu.VMEM((count, width), BF16),
                pltpu.VMEM((width, count), BF16),
                pltpu.VMEM((count, width), BF16),
                pltpu.VMEM((width, count), BF16),
                pltpu.VMEM((count, width), F32),
                pltpu.VMEM((count, 256), BF16),
                pltpu.VMEM((256, count), BF16),
                pltpu.VMEM((count, 640), BF16),
                pltpu.VMEM((count, 640), BF16),
            ],
        ),
        compiler_params=pltpu.CompilerParams(vmem_limit_bytes=VMEM_BYTES),
        name="attn_backward",
    )(length, tokens, grad_resid, context, seg, bx, by, gain, shift, weights, bias, offsets)


def offset_rows(table_x, table_y):
    half = BINS // 2
    first = LEVELS - half

    def spread(table):
        heads = table.shape[0]
        return jnp.concatenate(
            [
                jnp.broadcast_to(table[:, :1], (heads, first)),
                table,
                jnp.broadcast_to(table[:, -1:], (heads, 2 * LEVELS - first - BINS)),
            ],
            axis=1,
        )

    both = jnp.stack([spread(table_x), spread(table_y)], axis=1)
    return jnp.pad(both, ((0, 0), (0, 6), (0, 0)))


def fold_offsets(sums):
    half = BINS // 2
    start = LEVELS - 1 - half
    middle = sums[..., start + 1 : start + BINS - 1]
    low = jnp.sum(sums[..., : start + 1], axis=-1, keepdims=True)
    high = jnp.sum(sums[..., start + BINS - 1 :], axis=-1, keepdims=True)
    return jnp.concatenate([low, middle, high], axis=-1)


def local(
    tokens,
    cotangent,
    segment,
    box_x,
    box_y,
    page_tokens,
    gain_attn,
    shift_attn,
    w_query,
    b_query,
    w_key,
    w_value,
    b_value,
    table_x,
    table_y,
    w_attn_out,
    b_attn_out,
    gain_mlp,
    shift_mlp,
    w_in,
    b_in,
    w_out,
    b_out,
):
    pages, count = segment.shape
    width = tokens.shape[1]
    heads, size = b_query.shape
    inner = heads * size
    hidden = w_in.shape[1]
    n_dp = lax.axis_size("dp")
    n_tensor = lax.axis_size("tensor")
    dp_at = lax.axis_index("dp")
    page_at = lax.axis_index("tensor")

    w_attn = jnp.concatenate([w_query, w_key, w_value, w_attn_out.T], axis=1)
    qkv_bias = jnp.concatenate(
        [b_query.reshape(1, -1), jnp.zeros((1, inner), F32), b_value.reshape(1, -1)], axis=1
    )
    offsets = offset_rows(table_x, table_y)

    def gather(weight):
        piece = weight.shape[0] // n_dp
        own = lax.dynamic_slice_in_dim(weight, dp_at * piece, piece, 0)
        column = lax.all_gather(own, "tensor", axis=0)
        parts = lax.all_gather(column, "dp", axis=0)
        if n_dp != GROUP:
            parts = parts.reshape(GROUP, n_dp // GROUP, n_tensor, piece, -1)
            parts = jnp.swapaxes(parts, 1, 2).reshape(
                GROUP, n_tensor, weight.shape[0] // GROUP, -1
            )
        return parts

    full_attn = gather(w_attn)
    full_in = gather(w_in)
    full_out = gather(w_out)
    small = jnp.concatenate(
        [qkv_bias.reshape(-1), b_in.reshape(-1), offsets.reshape(-1)]
    )
    small = lax.all_gather(small, "tensor", axis=0)
    full_bias = small[:, : 3 * inner].reshape(n_tensor, 1, 3 * inner)
    full_b_in = small[:, 3 * inner : 3 * inner + hidden].reshape(n_tensor, 1, hidden)
    full_offsets = small[:, 3 * inner + hidden :].reshape((n_tensor,) + offsets.shape)

    row = lambda v: v.reshape(1, -1)
    context = attn_forward(
        page_tokens,
        tokens.reshape(pages, count, width),
        segment.reshape(pages, 1, count),
        box_x.reshape(pages, 1, count),
        box_y.reshape(pages, 1, count),
        row(gain_attn),
        row(shift_attn),
        w_attn[:, : 3 * inner],
        qkv_bias,
        offsets,
    )
    context = lax.all_to_all(context, "tensor", 0, 0, tiled=True)
    mine = lambda array, rows: lax.dynamic_slice_in_dim(array, page_at * rows, rows, 0)
    own_tokens = mine(tokens, count)
    layer_part, grad_resid, grads_mlp, rows_mlp, grad_b_in = mlp(
        own_tokens,
        mine(cotangent, count),
        context,
        full_attn[:, :, :, 3 * inner :],
        row(b_attn_out),
        row(gain_mlp),
        row(shift_mlp),
        full_in,
        full_b_in,
        full_out,
        row(b_out),
    )
    input_part, grads_attn, rows_attn, grad_bias, grad_tables = attn_backward(
        mine(page_tokens, 1),
        own_tokens,
        grad_resid,
        context,
        mine(segment, 1),
        mine(box_x, 1),
        mine(box_y, 1),
        row(gain_attn),
        row(shift_attn),
        full_attn,
        full_bias,
        full_offsets,
    )
    layer_out = lax.all_gather(layer_part, "tensor", axis=0, tiled=True)
    input_grad = lax.all_gather(input_part, "tensor", axis=0, tiled=True)

    def scatter(array):
        if n_dp != GROUP:
            rest = array.shape[1:-2]
            more = n_dp // GROUP
            array = array.reshape((GROUP,) + rest + (more, -1, array.shape[-1]))
            array = jnp.moveaxis(array, -3, 1).reshape((n_dp,) + rest + (-1, array.shape[-1]))
        array = lax.psum_scatter(array, "dp", scatter_dimension=0, tiled=False)
        return lax.psum_scatter(array, "tensor", scatter_dimension=0, tiled=False)

    sum_mlp = scatter(grads_mlp).astype(F32)
    sum_attn = scatter(grads_attn).astype(F32)
    vectors = jnp.concatenate([rows_attn[:2], rows_mlp[:4]], axis=0)
    vectors = jnp.swapaxes(vectors.reshape(6, n_dp, -1), 0, 1)
    vectors = jnp.broadcast_to(vectors[:, None], (n_dp, n_tensor) + vectors.shape[1:])
    tables = fold_offsets(grad_tables[:, :, :2, :])

    def by_dp(array):
        array = array.reshape(n_tensor, -1, n_dp, array.shape[-1] // n_dp)
        return jnp.moveaxis(array, 2, 0)

    pieces = [
        vectors.reshape(n_dp, n_tensor, -1),
        by_dp(grad_bias[:, 0].reshape(n_tensor, heads, size)).reshape(n_dp, n_tensor, -1),
        by_dp(grad_bias[:, 1].reshape(n_tensor, heads, size)).reshape(n_dp, n_tensor, -1),
        by_dp(tables[:, :, 0]).reshape(n_dp, n_tensor, -1),
        by_dp(tables[:, :, 1]).reshape(n_dp, n_tensor, -1),
        by_dp(grad_b_in.reshape((n_tensor,) + b_in.shape)).reshape(n_dp, n_tensor, -1),
    ]
    packed = jnp.concatenate(pieces, axis=2)
    packed = lax.psum_scatter(packed, "dp", scatter_dimension=0, tiled=False)
    packed = lax.psum_scatter(packed, "tensor", scatter_dimension=0, tiled=False)
    sizes = [p.shape[2] for p in pieces]
    starts = [sum(sizes[:i]) for i in range(len(sizes))]
    cut = [packed[s : s + n] for s, n in zip(starts, sizes)]
    sum_vectors = cut[0].reshape(6, -1)
    head_shape = (heads, -1)
    return (
        layer_out,
        input_grad,
        sum_vectors[0],
        sum_vectors[1],
        sum_attn[:, :inner],
        cut[1].reshape(head_shape),
        sum_attn[:, inner : 2 * inner],
        sum_attn[:, 2 * inner : 3 * inner],
        cut[2].reshape(head_shape),
        cut[3].reshape(head_shape),
        cut[4].reshape(head_shape),
        sum_attn[:, 3 * inner :].T,
        sum_vectors[4],
        sum_vectors[2],
        sum_vectors[3],
        sum_mlp[0],
        cut[5].reshape(b_in.shape[0], -1),
        sum_mlp[1].T,
        sum_vectors[5],
    )


def solution(mesh):
    split = P("tensor", None)
    return jax.shard_map(
        local,
        mesh=mesh,
        in_specs=(
            P("dp", None),
            P("dp", None),
            P("dp", None),
            P("dp", None),
            P("dp", None),
            P("dp"),
            P(),
            P(),
            P(None, "tensor"),
            split,
            P(None, "tensor"),
            P(None, "tensor"),
            split,
            split,
            split,
            split,
            P(),
            P(),
            P(),
            P(None, "tensor"),
            split,
            split,
            P(),
        ),
        out_specs=(
            P("dp", None),
            P("dp", None),
            P("dp"),
            P("dp"),
            P("dp", "tensor"),
            P("tensor", "dp"),
            P("dp", "tensor"),
            P("dp", "tensor"),
            P("tensor", "dp"),
            P("tensor", "dp"),
            P("tensor", "dp"),
            P("tensor", "dp"),
            P("dp"),
            P("dp"),
            P("dp"),
            P("dp", "tensor"),
            P("tensor", "dp"),
            P("tensor", "dp"),
            P("dp"),
        ),
        check_vma=False,
    )
```

time: 937 us -> 486 us (0.52)
  waiting for transfers between devices: 625 us -> 248 us
  matrix products: 154 us -> 0 us
  Pallas kernels: 0 us -> 83.7 us
  blocking collectives: 12.5 us -> 73.5 us
  other arithmetic: 65.4 us -> 8.07 us
    psum x3 -> x0, waiting for transfers between devices: 442 us -> none  [the longest x1 209 us: local(): mlp_total = lax.psum(mlp_part, 'tensor').astype(jnp.float32)]
    dot_general x71 -> x0, matrix products: 139 us -> none  [the longest x1 19.1 us: local(): jnp.einsum('td,fd->tf', cotangent, w_out, preferred_element_type=jnp.floa...]
    pallas_call x0 -> x3, Pallas kernels: none -> 83.7 us  [the longest x1 39.9 us: attn_backward(): pl.pallas_call(attn_backward_kernel, out_shape=(jax.ShapeDtypeStruct((cou...]
    all_gather x0 -> x3, blocking collectives: none -> 54.7 us  [gather(): column = lax.all_gather(own, 'tensor', axis=0)]
    all_gather x0 -> x5, waiting for transfers between devices: none -> 37.4 us  [the longest x3 37.4 us: gather(): parts = lax.all_gather(column, 'dp', axis=0)]
    reduce_sum x15 -> x2, other arithmetic: 32 us -> 1.86 us  [the longest x1 0.97 us: fold_offsets(): high = jnp.sum(sums[..., start + BINS - 1:], axis=-1, keepdims=True)]
    reduce_scatter x3 -> x4, waiting for transfers between devices: 131 us -> 152 us  [the longest x2 124 us: scatter(): array = lax.psum_scatter(array, 'dp', scatter_dimension=0, tiled=False)]
    convert_element_type x11 -> x2, other arithmetic: 22.3 us -> 1.93 us  [the longest x1 1 us: local(): sum_mlp = scatter(grads_mlp).astype(F32)]
  transfers between devices with their start and end apart: 9 -> 12, of which waited for: 9 -> 6; matrix products, arithmetic and copies ran while one was open for 8% -> 8% of each run, Pallas kernels for 0% -> 4%
where the time goes in v1:
time: 486 us; the launch traced here: 485 us
  waiting for transfers between devices  248 us (51%)
  Pallas kernels  83.7 us (17%)
  blocking collectives  73.5 us (15%)
  local copies, waits for them, and re-layouts  50.5 us (10%)
  between operations  16.4 us (3%)
  other arithmetic  8.07 us (2%)
    reduce_scatter x2, waiting for transfers between devices, scatter(): array = lax.psum_scatter(array, 'dp', scatter_dimension=0, tiled=False)  124 us
    unnamed x13, waiting for transfers between devices  56.3 us
    all_gather x3, blocking collectives, gather(): column = lax.all_gather(own, 'tensor', axis=0)  54.7 us
    pallas_call x1, Pallas kernels, attn_backward(): pl.pallas_call(attn_backward_kernel, out_shape=(jax.ShapeDtypeStruct((cou...  39.9 us
    all_gather x3, waiting for transfers between devices, gather(): parts = lax.all_gather(column, 'dp', axis=0)  37.4 us
    reduce_scatter x2, waiting for transfers between devices, scatter(): return lax.psum_scatter(array, 'tensor', scatter_dimension=0, tiled=False)  27.4 us
    pallas_call x1, Pallas kernels, mlp(): pl.pallas_call(mlp_kernel, out_shape=(jax.ShapeDtypeStruct((count, width)...  24.7 us
    pallas_call x1, Pallas kernels, attn_forward(): pl.pallas_call(attn_forward_kernel, out_shape=jax.ShapeDtypeStruct((pages...  19.1 us
  transfers between devices with their start and end apart: 12, of which 6 were waited for; matrix products, arithmetic and copies ran while one was open for 8% of the time, Pallas kernels for 4%

profile of v1, /device:TPU:0, one launch (start us, length us, event | category | flops | bytes accessed | tf_op | source)
XLA Modules:
  0.0 485.3 jit_solution(13454513871565424524)
XLA Ops:
  14.2 1.3 fusion.7
  21.7 20.5 %all-gather = bf16[384,768]{1,0:T(8,128)(2,1)} all-gather(bf16[96,768]{1,0:T(8,128)(2,1)S(1)} %fusion.2), channel_id=2, replica_groups=mesh['dp'=8,'tensor'=4] {'tensor'}, dimensions={0}, use_global_device_ids=true | all-gather | bytes 737280 | tf_op jit(solution)/shard_map/all_gather | solution.py:551
  42.3 17.3 %all-gather.5 = bf16[384,768]{1,0:T(8,128)(2,1)} all-gather(bf16[96,768]{1,0:T(8,128)(2,1)S(1)} %constant_dynamic-slice_fusion.3), channel_id=7, replica_groups=mesh['dp'=8,'tensor'=4] {'tensor'}, dimensions={0}, use_global_device_ids=true | all-gather | bytes 737280 | tf_op jit(solution)/shard_map/all_gather | solution.py:551
  60.6 16.9 %all-gather.2 = bf16[384,768]{1,0:T(8,128)(2,1)} all-gather(bf16[96,768]{1,0:T(8,128)(2,1)S(1)} %constant_dynamic-slice_fusion.4), channel_id=4, replica_groups=mesh['dp'=8,'tensor'=4] {'tensor'}, dimensions={0}, use_global_device_ids=true | all-gather | bytes 737280 | tf_op jit(solution)/shard_map/all_gather | solution.py:551
  80.6 1.3 pad_maximum_fusion.weights
  81.9 19.1 %attn_forward.1 = bf16[4,512,192]{2,1,0:T(8,128)(2,1)} custom-call(s32[4]{0:T(128)} %lengths.1, bf16[4,512,768]{2,1,0:T(8,128)(2,1)} %bitcast.81, s32[4,1,512]{2,1,0:T(1,128)} %reshape.164.seg, s32[4,1,512]{2,1,0:T(1,128)} %reshape.165.bx, s32[4,1,512]{2,1,0:T(1,128)} %reshape.166.by, f32[1,768]{1,0:T(1,128)} %reshape.167.gain, f32[1,768]{1,0:T(1,128)} %reshape.168.shift, ...), custom_call_target="tpu_custom_call" | custom-call | tf_op jit(solution)/shard_map/attn_forward/pallas_call | solution.py:138
  101.0 2.2 copy.80
  103.2 4.3 all-to-all-start
  111.7 2.7 constant_dynamic-slice_fusion.5
  117.5 3.1 all-to-all-done
  120.7 1.3 copy.85.context
  121.9 3.3 slice.163.w_attn
  125.2 37.4 %all-gather.19.cloned.1.call-done = bf16[32,96,768]{2,1,0:T(8,128)(2,1)} async-done(((bf16[4,96,768]{2,1,0:T(8,128)(2,1)}), bf16[32,96,768]{2,1,0:T(8,128)(2,1)}) %all-gather.19.cloned.1.call-update) | async-done | bytes 4718608 | tf_op jit(solution)/shard_map/all_gather | solution.py:552
  162.6 24.7 %mlp.1 = (bf16[512,768]{1,0:T(8,128)(2,1)}, f32[512,768]{1,0:T(8,128)}, bf16[8,4,2,96,768]{4,3,2,1,0:T(8,128)(2,1)}, f32[8,768]{1,0:T(8,128)}, f32[4,1,768]{2,1,0:T(1,128)}) custom-call(bf16[512,768]{1,0:T(8,128)(2,1)} %get-tuple-element.128.tokens, bf16[512,768]{1,0:T(8,128)(2,1)} %get-tuple-element.127.cotangent, bf16[4,512,192]{2,1,0:T(8,128)(2,1)} %copy.85.context, ...), custom_call_target="tpu_custom_call" | custom-call | tf_op jit(solution)/shard_map/mlp/pallas_call | solution.py:248
  187.3 39.9 %attn_backward.1 = (bf16[512,768]{1,0:T(8,128)(2,1)}, bf16[8,4,96,768]{3,2,1,0:T(8,128)(2,1)}, f32[8,768]{1,0:T(8,128)}, f32[4,8,192]{2,1,0:T(8,128)}, f32[4,3,8,256]{3,2,1,0:T(8,128)}) custom-call(s32[1]{0:T(128)} %dynamic_slice.32.lengths, bf16[512,768]{1,0:T(8,128)(2,1)} %get-tuple-element.128.tokens, f32[512,768]{1,0:T(8,128)} %get-tuple-element.30.grad_resid, ...), custom_call_target="tpu_custom_call" | custom-call | tf_op jit(solution)/shard_map/attn_backward/pallas_call | solution.py:430
  236.6 44.4 %reduce-scatter.5.cloned.1.call-done = bf16[1,4,96,768]{3,2,1,0:T(8,128)(2,1)} async-done(((bf16[8,4,96,768]{3,2,1,0:T(8,128)(2,1)}), bf16[1,4,96,768]{3,2,1,0:T(8,128)(2,1)}) %reduce-scatter.5.cloned.1.call-update) | async-done | bytes 589840 | tf_op jit(solution)/shard_map/reduce_scatter | solution.py:623
  281.2 79.8 %reduce-scatter.9.cloned.1.call-done = bf16[1,4,2,96,768]{4,3,2,1,0:T(8,128)(2,1)} async-done(((bf16[8,4,2,96,768]{4,3,2,1,0:T(8,128)(2,1)}), bf16[1,4,2,96,768]{4,3,2,1,0:T(8,128)(2,1)}) %reduce-scatter.9.cloned.1.call-update) | async-done | bytes 1179664 | tf_op jit(solution)/shard_map/reduce_scatter | solution.py:623
  361.5 54.1 %all-reduce.9.cloned.1.call-done = f32[8,4,768]{2,1,0:T(4,128)} async-done(((f32[8,4,768]{2,1,0:T(4,128)}), f32[8,4,768]{2,1,0:T(4,128)}) %all-reduce.9.cloned.1.call-update) | async-done | bytes 98320
  415.6 1.4 dynamic-slice_bitcast_fusion
  417.0 18.8 %all-reduce.3 = f32[4,768]{1,0:T(4,128)S(1)} all-reduce(f32[4,768]{1,0:T(4,128)S(1)} %dynamic-slice_bitcast_fusion), channel_id=10, replica_groups=mesh['dp'=8,'tensor'=4] {'tensor'}, use_global_device_ids=true, to_apply=%region_3.4.clone | all-reduce | flops 3072 | bytes 24576
  439.1 1.2 dynamic-slice_bitcast_fusion.1
  443.4 27.4 %reduce-scatter.11.cloned.1.call-done = bf16[1,2,96,768]{3,2,1,0:T(8,128)(2,1)} async-done(((bf16[4,2,96,768]{3,2,1,0:T(8,128)(2,1)}), bf16[1,2,96,768]{3,2,1,0:T(8,128)(2,1)}) %reduce-scatter.11.cloned.1.call-update) | async-done | bytes 294928 | tf_op jit(solution)/shard_map/reduce_scatter | solution.py:624
  472.6 3.9 copy.129
  476.5 1.7 copy.130
  (161 shorter events, 41.1 us)
Async XLA Ops:
  8.0 34.3 %copy-start = (bf16[768,768]{1,0:T(8,128)(2,1)S(1)}, bf16[768,768]{1,0:T(8,128)(2,1)}, u32[]{:S(2)}) copy-start(bf16[768,768]{1,0:T(8,128)(2,1)} %param.44) | copy-start | bytes 3538948
  8.0 13.2 %copy-start.4 = (bf16[768,192]{0,1:T(8,128)(2,1)S(1)}, bf16[768,192]{0,1:T(8,128)(2,1)}, u32[]{:S(2)}) copy-start(bf16[768,192]{0,1:T(8,128)(2,1)} %param.34) | copy-start | bytes 884740
  8.1 13.3 %copy-start.5 = (bf16[192,768]{1,0:T(8,128)(2,1)S(1)}, bf16[192,768]{1,0:T(8,128)(2,1)}, u32[]{:S(2)}) copy-start(bf16[192,768]{1,0:T(8,128)(2,1)} %param.38) | copy-start | bytes 884740
  8.1 106.3 %all-reduce.7.cloned.1.call-start = ((), (), s32[]{:S(2)}) async-start(), calls=%async_computation.14 | async-start | bytes 245760
  18.9 103.1 %all-gather.17.cloned.1.call-start = ((), (), s32[]{:S(2)}) async-start(), calls=%async_computation.11 | async-start | bytes 5308416 | tf_op jit(solution)/shard_map/all_gather | solution.py:552
  42.2 35.4 %copy-start.11 = (f32[768]{0:T(1024)S(1)}, f32[768]{0:T(1024)}, u32[]{:S(2)}) copy-start(f32[768]{0:T(1024)} %param.29) | copy-start | bytes 9220
  42.2 36.0 %copy-start.12 = (f32[768]{0:T(1024)S(1)}, f32[768]{0:T(1024)}, u32[]{:S(2)}) copy-start(f32[768]{0:T(1024)} %param.30) | copy-start | bytes 9220
  42.2 36.6 %copy-start.6 = (s32[4,512]{1,0:T(4,128)S(1)}, s32[4,512]{1,0:T(4,128)}, u32[]{:S(2)}) copy-start(s32[4,512]{1,0:T(4,128)} %param.25) | copy-start | bytes 24580
  42.2 37.2 %copy-start.7 = (s32[4,512]{1,0:T(4,128)S(1)}, s32[4,512]{1,0:T(4,128)}, u32[]{:S(2)}) copy-start(s32[4,512]{1,0:T(4,128)} %param.26) | copy-start | bytes 24580
  42.2 37.8 %copy-start.8 = (s32[4,512]{1,0:T(4,128)S(1)}, s32[4,512]{1,0:T(4,128)}, u32[]{:S(2)}) copy-start(s32[4,512]{1,0:T(4,128)} %param.27) | copy-start | bytes 24580
  42.2 83.0 %all-gather.21.cloned.1.call-start = ((), (), s32[]{:S(2)}) async-start(), calls=%async_computation.13 | async-start | bytes 5308416 | tf_op jit(solution)/shard_map/all_gather | solution.py:552
  59.6 102.9 %all-gather.19.cloned.1.call-start = ((), (), s32[]{:S(2)}) async-start(), calls=%async_computation.12 | async-start | bytes 5308416 | tf_op jit(solution)/shard_map/all_gather | solution.py:552
  101.0 7.8 %copy-start.14 = (f32[768]{0:T(1024)S(1)}, f32[768]{0:T(1024)}, u32[]{:S(2)}) copy-start(f32[768]{0:T(1024)} %param.40) | copy-start | bytes 9220
  101.0 8.3 %copy-start.15 = (f32[768]{0:T(1024)S(1)}, f32[768]{0:T(1024)}, u32[]{:S(2)}) copy-start(f32[768]{0:T(1024)} %param.41) | copy-start | bytes 9220
  101.0 8.9 %copy-start.16 = (f32[768]{0:T(1024)S(1)}, f32[768]{0:T(1024)}, u32[]{:S(2)}) copy-start(f32[768]{0:T(1024)} %param.45) | copy-start | bytes 9220
  103.2 17.4 %all-to-all-start = ((bf16[4,512,192]{1,2,0:T(8,128)(2,1)}), bf16[4,512,192]{1,2,0:T(8,128)(2,1)S(1)}, u32[]{:S(2)}, u32[]{:S(2)}) async-start(bf16[4,512,192]{1,2,0:T(8,128)(2,1)} %copy.80), calls=%async_computation | async-start | bytes 1572864 | tf_op jit(solution)/shard_map/all_to_all | solution.py:584
  107.6 173.5 %reduce-scatter.5.cloned.1.call-start = ((), (), s32[]{:S(2)}) async-start(), calls=%async_computation.7 | async-start | bytes 5308416 | tf_op jit(solution)/shard_map/reduce_scatter | solution.py:623
  227.2 133.7 %reduce-scatter.9.cloned.1.call-start = ((), (), s32[]{:S(2)}) async-start(), calls=%async_computation.9 | async-start | bytes 10616832 | tf_op jit(solution)/shard_map/reduce_scatter | solution.py:623
  227.9 187.7 %all-reduce.9.cloned.1.call-start = ((), (), s32[]{:S(2)}) async-start(), calls=%async_computation.15 | async-start | bytes 196608
  234.2 126.7 %copy-start.18 = (u32[32]{0:T(128)S(1)}, u32[32]{0:T(128)}, u32[]{:S(2)}) copy-start(u32[32]{0:T(128)} %constant.44) | copy-start | bytes 388
  235.1 205.9 %all-gather.15.cloned.1.call-start = ((), (), s32[]{:S(2)}) async-start(), calls=%async_computation.6 | async-start | bytes 3932160 | tf_op jit(solution)/shard_map/all_gather | solution.py:615
  235.9 205.1 %all-gather.13.cloned.1.call-start = ((), (), s32[]{:S(2)}) async-start(), calls=%async_computation.5 | async-start | bytes 3932160 | tf_op jit(solution)/shard_map/all_gather | solution.py:614
  236.6 204.4 %reduce-scatter.7.cloned.1.call-start = ((), (), s32[]{:S(2)}) async-start(), calls=%async_computation.8 | async-start | bytes 737280 | tf_op jit(solution)/shard_map/reduce_scatter | solution.py:624
  281.1 189.7 %reduce-scatter.11.cloned.1.call-start = ((), (), s32[]{:S(2)}) async-start(), calls=%async_computation.10 | async-start | bytes 1474560 | tf_op jit(solution)/shard_map/reduce_scatter | solution.py:624
  (7 other events, 35.3 us)
Sparse Core Ops, SparseCore 0:
  19.0 38.2 all-reduce.6
  238.2 63.5 all-gather.14
  303.4 62.1 all-gather.12
Sparse Core Ops, SparseCore 1:
  42.3 38.8 all-gather.16
  83.1 38.7 all-gather.20
  123.8 38.7 all-gather.18
  227.3 53.8 reduce-scatter.4
  284.6 76.3 reduce-scatter.8
  364.6 51.0 all-reduce.8
  417.9 22.9 reduce-scatter.6
  443.2 27.5 reduce-scatter.10
